TPU v7x, 768 devices: a whole 4x8x12 slice. The times are simulated.
768 devices in a mesh: dap: 96 (over x, z, y_lo), section: 8 (over y_hi, core).
Axes of the slice: x: 4, y: 8 (y_hi: 4, y_lo: 2; y = y_hi * 2 + y_lo), z: 12, core: 2. Of those that a mesh axis runs over, the one named last changes fastest.
Arguments:
- alignment_state_new: float32 [8, 384, 384, 256], P('section', 'dap'), may hold values from -8 to 8
- residue_grid_new: float32 [8, 384, 384, 128], P('section', 'dap'), may hold values from -8 to 8
- stacked_projection_weights: bfloat16 [8, 256, 1024], P('section'), may hold values from -0.375 to 0.375
- outgoing_weight_matrix: bfloat16 [8, 256, 256], P('section'), may hold values from -0.375 to 0.375
- grid_logit_matrix: bfloat16 [8, 128, 8], P('section'), may hold values from -14 to 14, as said below
- layernorm_gain_vector: float32 [8, 256], P('section'), may hold values from 0.5 to 1.5
- grid_scale_factor: float32 [8, 128], P('section'), may hold values from 0.5 to 1.5
- sigmoid_offset: float32 [8, 256], P('section'), may hold values from -1 to 2
- outgoing_bias_vector: float32 [8, 256], P('section'), may hold values from -3 to 3
Outputs:
- alignment_after_attention: float32 [8, 384, 384, 256], P('section', 'dap')
- grid_state_handed: float32 [8, 384, 384, 128], P('section', 'dap')
Inputs may be any that keep to these rules, and one draw needn't show every extreme that they name: `grid_logit_matrix`: pair-bias projection weights.
All inputs are finite; a program needn't handle non-finite values.
Results may differ from a plain program's by a relative error of at most 0.0053.
Values may be sent and summed in bfloat16 or wider, within the bound.
A program may use at most 128 MiB of HBM per device.

v0:
```python
import jax
import jax.numpy as jnp
from jax import lax
from jax.sharding import PartitionSpec as P

epsilon = 1e-05


def passed_along(value, axis, steps):
    count = lax.axis_size(axis)
    pairs = [(source, (source + steps) % count) for source in range(count)]
    return lax.ppermute(value, axis, pairs)


def standardize_features(values, gain):
    center = values - jnp.mean(values, axis=-1, keepdims=True)
    spread = jnp.mean(center * center, axis=-1, keepdims=True)
    return center * lax.rsqrt(spread + epsilon) * gain


def pair_bias(pair_rows, weight_rows, gain_row):
    pair_norm = standardize_features(pair_rows, gain_row).astype(jnp.bfloat16)
    return jnp.einsum(
        "ijc,ch->hij", pair_norm, weight_rows, preferred_element_type=jnp.float32
    ).astype(jnp.bfloat16)


def body(
    alignment_state_new,
    residue_grid_new,
    stacked_projection_weights,
    outgoing_weight_matrix,
    grid_logit_matrix,
    layernorm_gain_vector,
    grid_scale_factor,
    sigmoid_offset,
    outgoing_bias_vector,
):
    arrived_alignment_lines, arrived_grid_lines = passed_along(
        (alignment_state_new, residue_grid_new), "section", 1
    )
    alignment_arriving = arrived_alignment_lines[0]
    aligned_lines, crop_length_value, feature_depth = alignment_arriving.shape
    heads = grid_logit_matrix.shape[2]
    width = stacked_projection_weights.shape[2] // 4
    head_dim = width // heads
    score_scale = 1.0 / head_dim**0.5
    alignment_standardized = standardize_features(
        alignment_arriving, layernorm_gain_vector[0]
    ).astype(jnp.bfloat16)
    mapped_lines = jnp.dot(
        alignment_standardized.reshape(aligned_lines * crop_length_value, feature_depth),
        stacked_projection_weights[0],
        preferred_element_type=jnp.float32,
    )
    mapped_lines = mapped_lines.reshape(aligned_lines, crop_length_value, 4 * width)
    queries = (
        mapped_lines[..., :width]
        .astype(jnp.bfloat16)
        .reshape(aligned_lines, crop_length_value, heads, head_dim)
    )
    key_rows = (
        mapped_lines[..., width : 2 * width]
        .astype(jnp.bfloat16)
        .reshape(aligned_lines, crop_length_value, heads, head_dim)
    )
    val_rows = (
        mapped_lines[..., 2 * width : 3 * width]
        .astype(jnp.bfloat16)
        .reshape(aligned_lines, crop_length_value, heads, head_dim)
    )
    gates = jax.nn.sigmoid(mapped_lines[..., 3 * width :] + sigmoid_offset[0])
    weight_out = outgoing_weight_matrix[0]
    local_bias = pair_bias(arrived_grid_lines[0], grid_logit_matrix[0], grid_scale_factor[0])
    bias_rows = lax.all_gather(local_bias, "dap", axis=1, tiled=True)
    count = bias_rows.shape[1]
    scores = (
        jnp.einsum("sihd,sjhd->shij", queries, key_rows, preferred_element_type=jnp.float32)
        * score_scale
    )
    scores = scores + bias_rows[None].astype(jnp.float32)
    probs = jax.nn.softmax(scores, axis=-1).astype(jnp.bfloat16)
    attended = jnp.einsum(
        "shij,sjhd->sihd", probs, val_rows, preferred_element_type=jnp.float32
    ).reshape(aligned_lines, count, width)
    gated = (attended * gates).astype(jnp.bfloat16)
    mapped = jnp.dot(
        gated.reshape(aligned_lines * count, width), weight_out, preferred_element_type=jnp.float32
    )
    line_increment = mapped.reshape(aligned_lines, count, feature_depth)
    alignment_after_attention = alignment_arriving + (line_increment + outgoing_bias_vector[0])
    return (alignment_after_attention[None], arrived_grid_lines)


def solution(mesh):
    in_specs = (
        P("section", "dap", None, None),
        P("section", "dap", None, None),
        P("section", None, None),
        P("section", None, None),
        P("section", None, None),
        P("section", None),
        P("section", None),
        P("section", None),
        P("section", None),
    )
    out_specs = (P("section", "dap", None, None), P("section", "dap", None, None))
    return jax.shard_map(body, mesh=mesh, in_specs=in_specs, out_specs=out_specs, check_vma=False)
```

profile of v0, /device:TPU:16, one launch (start us, length us, event | category | flops | bytes accessed | tf_op | source)
XLA Modules:
  0.0 542.3 jit_solution(8692547549826974979)
XLA Ops:
  7.2 0.0 copy-start
  7.2 0.0 copy-start.3
  7.2 0.0 copy-start.1
  7.2 0.0 all-gather.2.cloned.1.call-start
  7.2 2.1 collective-permute-start.1
  9.3 21.0 %collective-permute-done.1 = f32[1,4,384,128]{3,2,1,0:T(8,128)S(1)} collective-permute-done((f32[1,4,384,128]{3,2,1,0:T(8,128)}, f32[1,4,384,128]{3,2,1,0:T(8,128)S(1)}, u32[]{:S(2)}, u32[]{:S(2)}) %collective-permute-start.1) | collective-permute-done | bytes 786464 | tf_op jit(solution)/shard_map/ppermute | solution.py:12
  30.3 0.3 reduce_sum.47
  30.6 0.5 fusion.21
  31.1 0.0 copy-done.3
  31.1 0.0 copy-done.1
  31.1 1.2 fusion.16
  32.3 0.0 all-gather.2.cloned.1.call-update
  32.3 0.0 copy-start.2
  32.3 2.3 collective-permute-start
  34.6 35.1 %collective-permute-done = f32[1,4,384,256]{3,2,1,0:T(8,128)S(1)} collective-permute-done((f32[1,4,384,256]{3,2,1,0:T(8,128)}, f32[1,4,384,256]{3,2,1,0:T(8,128)S(1)}, u32[]{:S(2)}, u32[]{:S(2)}) %collective-permute-start) | collective-permute-done | bytes 1572896 | tf_op jit(solution)/shard_map/ppermute | solution.py:12
  69.8 0.3 reduce_sum.45
  70.1 0.5 fusion.13
  70.6 0.0 copy-done
  70.6 0.0 copy-done.2
  70.6 3.3 fusion.38
  73.9 1.6 fusion.37
  75.5 2.3 copy.25
  77.8 2.3 copy.24
  80.1 2.3 copy.23
  82.4 419.5 %all-gather.2.cloned.1.call-done = bf16[8,384,384]{2,0,1:T(8,128)(2,1)} async-done(((bf16[8,4,384]{2,0,1:T(8,128)(2,1)}), bf16[8,384,384]{2,0,1:T(8,128)(2,1)}) %all-gather.2.cloned.1.call-update) | async-done | bytes 2359312 | tf_op jit(solution)/shard_map/all_gather | solution.py:75
  501.9 5.1 copy.26
  507.0 11.6 %fusion.39 = (f32[4,8,384]{2,1,0:T(8,128)S(1)}, f32[4,8,384,384]{2,3,1,0:T(8,128)}) fusion(f32[8,384,384]{1,2,0:T(8,128)} %copy.26, bf16[4,384,8,32]{1,3,2,0:T(8,128)(2,1)} %bitcast.59, bf16[4,384,8,32]{1,3,2,0:T(8,128)(2,1)} %bitcast.57), kind=kOutput, calls=%fused_computation.49 | convolution fusion | flops 320864640 | bytes 25214976 | tf_op jit(solution)/shard_map/sub | solution.py:82
  518.6 9.3 %fusion.4 = f32[4,8,32,384]{3,2,1,0:T(8,128)} fusion(bf16[4,384,8,32]{1,3,2,0:T(8,128)(2,1)} %bitcast.58, f32[4,8,384,384]{2,3,1,0:T(8,128)} %get-tuple-element.8, f32[4,8,384]{2,1,0:T(8,128)S(1)} %get-tuple-element.7), kind=kOutput, calls=%fused_computation.7 | convolution fusion | flops 311427072 | bytes 21282816 | tf_op jit(solution)/shard_map/shij,sjhd->sihd/dot_general | solution.py:83
  527.9 3.1 copy.28
  530.9 0.0 copy-done.4
  530.9 3.6 fusion.14
  534.6 0.9 copy.31
  (9 shorter events, 0.0 us)
Async XLA Ops:
  7.2 63.4 %copy-start = (bf16[1,256,1024]{2,1,0:T(8,128)(2,1)S(1)}, bf16[1,256,1024]{2,1,0:T(8,128)(2,1)}, u32[]{:S(2)}) copy-start(bf16[1,256,1024]{2,1,0:T(8,128)(2,1)} %param.11) | copy-start | bytes 1572868
  7.2 23.9 %copy-start.3 = (f32[1,128]{1,0:T(1,128)S(1)}, f32[1,128]{1,0:T(1,128)}, u32[]{:S(2)}) copy-start(f32[1,128]{1,0:T(1,128)} %param.15) | copy-start | bytes 1540
  7.2 23.9 %copy-start.1 = (bf16[1,128,8]{1,2,0:T(8,128)(2,1)S(1)}, bf16[1,128,8]{1,2,0:T(8,128)(2,1)}, u32[]{:S(2)}) copy-start(bf16[1,128,8]{1,2,0:T(8,128)(2,1)} %param.13) | copy-start | bytes 6148
  7.2 494.7 %all-gather.2.cloned.1.call-start = ((), (), s32[]{:S(2)}) async-start(), calls=%async_computation | async-start | bytes 2383872 | tf_op jit(solution)/shard_map/all_gather | solution.py:75
  7.2 23.0 %collective-permute-start.1 = (f32[1,4,384,128]{3,2,1,0:T(8,128)}, f32[1,4,384,128]{3,2,1,0:T(8,128)S(1)}, u32[]{:S(2)}, u32[]{:S(2)}) collective-permute-start(f32[1,4,384,128]{3,2,1,0:T(8,128)} %param.10), channel_id=1, source_target_pairs={{0,1},{1,2},{2,3},{3,4},{4,5},{5,6},{6,7},{7,0},{8,9},{9,10},{10,1... | collective-permute-start | bytes 2359304 | tf_op jit(solution)/shard_map/ppermute | solution.py:12
  32.3 38.3 %copy-start.2 = (f32[1,256]{1,0:T(1,128)S(1)}, f32[1,256]{1,0:T(1,128)}, u32[]{:S(2)}) copy-start(f32[1,256]{1,0:T(1,128)} %param.14) | copy-start | bytes 3076
  32.3 37.4 %collective-permute-start = (f32[1,4,384,256]{3,2,1,0:T(8,128)}, f32[1,4,384,256]{3,2,1,0:T(8,128)S(1)}, u32[]{:S(2)}, u32[]{:S(2)}) collective-permute-start(f32[1,4,384,256]{3,2,1,0:T(8,128)} %param.9), channel_id=1, source_target_pairs={{0,1},{1,2},{2,3},{3,4},{4,5},{5,6},{6,7},{7,0},{8,9},{9,10},{10,1... | collective-permute-start | bytes 4718600 | tf_op jit(solution)/shard_map/ppermute | solution.py:12
  527.8 3.1 copy-start.4
  527.9 3.1 copy-start.5
  527.9 3.1 copy-start.6
Sparse Core Ops, SparseCore 0:
  32.4 469.4 all-gather.1
where the time goes:
time: 543 us; the launch traced here: 542 us
  waiting for transfers between devices  476 us (88%)
  matrix products  28.9 us (5%)
  local copies, waits for them, and re-layouts  17.6 us (3%)
  between operations  14.1 us (3%)
    all_gather x1, waiting for transfers between devices, body(): bias_rows = lax.all_gather(local_bias, 'dap', axis=1, tiled=True)  420 us
    ppermute x2, waiting for transfers between devices, passed_along(): return lax.ppermute(value, axis, pairs)  56.1 us
    sub x1, matrix products, body(): probs = jax.nn.softmax(scores, axis=-1).astype(jnp.bfloat16)  11.6 us
  transfers between devices with their start and end apart: 3, of which 3 were waited for; matrix products, arithmetic and copies ran while one was open for 2% of the time, Pallas kernels for 0%

commit v1 on v0

v1 whole, which is shorter than its diff:
```python
import functools

import jax
import jax.numpy as jnp
from jax import lax
from jax.experimental import pallas as pl
from jax.experimental.pallas import tpu as pltpu
from jax.sharding import PartitionSpec as P

EPSILON = 1e-05
MESH = pl.DeviceIdType.MESH
BF16 = jnp.bfloat16
F32 = jnp.float32
HALF = 128


def standardize(values, gain):
    center = values - jnp.mean(values, axis=-1, keepdims=True)
    spread = jnp.mean(center * center, axis=-1, keepdims=True)
    return center * lax.rsqrt(spread + EPSILON) * gain


def attend_row(x, bias, weights, w_out, gain, offset, out_bias, scratch, heads, dim):
    q_sc, k_sc, v_sc, gate_sc, gated_sc = scratch
    n, width = x.shape
    per_half = HALF // dim
    normed = standardize(x, gain).astype(BF16)
    member = lax.broadcasted_iota(jnp.int32, (n, HALF), 1) // dim

    def project(block):
        return jnp.dot(
            normed, weights[:, block * width : (block + 1) * width], preferred_element_type=F32
        )

    q_sc[...] = (project(0) * (1.0 / dim**0.5)).astype(BF16)
    keys = project(1)
    values = project(2)
    for h in range(heads):
        lanes = slice(h // per_half * HALF, (h // per_half + 1) * HALF)
        mine = member == h % per_half
        k_sc[h * n : (h + 1) * n, :] = jnp.where(mine, keys[:, lanes], 0.0).astype(BF16)
        v_sc[h * n : (h + 1) * n, :HALF] = jnp.where(mine, values[:, lanes], 0.0).astype(BF16)
    gate_sc[...] = jax.nn.sigmoid(project(3) + offset)
    for half in range(width // HALF):
        lanes = slice(half * HALF, (half + 1) * HALF)
        queries = q_sc[:, lanes]
        total = None
        for pair in range(per_half // 2):
            h = half * per_half + pair * 2
            scores = lax.dot_general(
                queries,
                k_sc[h * n : (h + 2) * n, :],
                (((1,), (1,)), ((), ())),
                preferred_element_type=F32,
            )
            probs = []
            for u in range(2):
                own = bias[:, :, (h + u) * n : (h + u + 1) * n].astype(F32).reshape(n, n)
                shifted = scores[:, u * n : (u + 1) * n] + own
                top = jnp.max(shifted, axis=-1, keepdims=True)
                probs.append(jnp.exp(shifted - top).astype(BF16))
            part = jnp.dot(
                jnp.concatenate(probs, axis=-1),
                v_sc[h * n : (h + 2) * n, :],
                preferred_element_type=F32,
            )
            total = part if total is None else total + part
        gated_sc[:, lanes] = (total[:, :HALF] / total[:, HALF:] * gate_sc[:, lanes]).astype(BF16)
    return x + (jnp.dot(gated_sc[...], w_out, preferred_element_type=F32) + out_bias)


def kernel(
    nx,
    nz,
    ns,
    heads,
    dim,
    msa_hbm,
    pair_hbm,
    weights_hbm,
    w_out_hbm,
    logit_ref,
    gain_ref,
    pair_gain_ref,
    offset_ref,
    out_bias_ref,
    out_hbm,
    pair_out_hbm,
    x_sc,
    pair_sc,
    w_sc,
    wo_sc,
    next_logit,
    next_gain,
    shard,
    stage,
    bias,
    q_sc,
    k_sc,
    v_sc,
    gate_sc,
    gated_sc,
    local_sem,
    w_send,
    w_recv,
    b_send,
    b_recv,
    zr_send,
    zr_recv,
    zl_send,
    zl_recv,
    xr_send,
    xr_recv,
    xl_send,
    xl_recv,
    m_send,
    m_recv,
    p_send,
    p_recv,
):
    rows, n = x_sc.shape[0], x_sc.shape[1]
    n_right = nz // 2
    n_left = nz - 1 - n_right
    d = lax.axis_index("dap")
    s = lax.axis_index("section")
    ndap = nx * nz * 2
    x = lax.div(d, 2 * nz)
    z = lax.rem(lax.div(d, 2), nz)
    low = lax.rem(d, 2)
    base = d - 2 * z
    z_right = base + 2 * lax.rem(z + 1, nz)
    z_left = base + 2 * lax.rem(z + nz - 1, nz)
    x_right = lax.rem(d + 2 * nz, ndap)
    x_left = lax.rem(d + ndap - 2 * nz, ndap)
    other = d + 1 - 2 * low
    s_next = lax.rem(s + 1, ns)
    s_prev = lax.rem(s + ns - 1, ns)

    def slot(dx, dz):
        return lax.rem(x + dx + nx, nx) * nz + lax.rem(z + dz + nz, nz)

    pair_in = pltpu.make_async_copy(pair_hbm.at[0], pair_sc, local_sem.at[0])
    w_in = pltpu.make_async_copy(weights_hbm.at[0], w_sc, local_sem.at[1])
    wo_in = pltpu.make_async_copy(w_out_hbm.at[0], wo_sc, local_sem.at[2])
    pair_in.start()
    w_in.start()
    wo_in.start()

    barrier = pltpu.get_barrier_semaphore()
    peers = (
        (z_right, s),
        (z_left, s),
        (x_right, s),
        (x_left, s),
        (d, s_next),
        (d, s_prev),
        (other, s_next),
        (other, s_prev),
    )
    for peer in peers:
        pl.semaphore_signal(barrier, inc=1, device_id=peer, device_id_type=MESH)
    pl.semaphore_wait(barrier, len(peers))

    def remote(src, dst, send, recv, peer):
        return pltpu.make_async_remote_copy(
            src_ref=src,
            dst_ref=dst,
            send_sem=send,
            recv_sem=recv,
            device_id=peer,
            device_id_type=MESH,
        )

    logit_copy = remote(logit_ref, next_logit, w_send.at[0], w_recv.at[0], (d, s_prev))
    gain_copy = remote(pair_gain_ref, next_gain, w_send.at[1], w_recv.at[1], (d, s_prev))
    logit_copy.start()
    gain_copy.start()

    def msa_copy(r):
        return remote(msa_hbm.at[0, r], x_sc.at[r], m_send.at[r], m_recv.at[r], (d, s_next))

    msa_copy(0).start()

    pair_in.wait()
    logit_copy.wait_recv()
    gain_copy.wait_recv()
    logits = next_logit[...]
    for r in range(rows):
        normed = standardize(pair_sc[r], next_gain[...]).astype(BF16)
        shard_row = lax.dot_general(
            logits, normed, (((1,), (1,)), ((), ())), preferred_element_type=F32
        )
        for h in range(heads):
            shard[r : r + 1, h * n : (h + 1) * n] = shard_row[h : h + 1, :]

    def shard_copy(index, row, peer):
        return remote(shard, stage.at[row], b_send.at[index], b_recv.at[row], peer)

    shard_copy(0, low, (d, s_next)).start()
    shard_copy(1, low, (other, s_next)).start()
    for r in range(1, rows):
        msa_copy(r).start()
    shard_copy(0, 0, (d, s_next)).wait_recv()
    shard_copy(1, 1, (other, s_next)).wait_recv()
    bias[slot(0, 0)] = jnp.concatenate([stage[0], stage[1]], axis=0).astype(BF16)

    def z_right_copy(t, block):
        return remote(bias.at[block], bias.at[block], zr_send.at[t], zr_recv.at[t], (z_right, s))

    def z_left_copy(t, block):
        return remote(bias.at[block], bias.at[block], zl_send.at[t], zl_recv.at[t], (z_left, s))

    def x_right_copy(t, block):
        return remote(bias.at[block], bias.at[block], xr_send.at[t], xr_recv.at[t], (x_right, s))

    def x_left_copy(t, block):
        return remote(bias.at[block], bias.at[block], xl_send.at[t], xl_recv.at[t], (x_left, s))

    own = slot(0, 0)
    z_right_copy(0, own).start()
    z_left_copy(0, own).start()
    x_right_copy(0, own).start()
    x_left_copy(0, own).start()

    def pass_right(t):
        block = slot(-1, -t)
        x_right_copy(t, block).wait_recv()
        x_right_copy(nz + t - 1, block).start()

    def pass_left(t):
        block = slot(1, t)
        x_left_copy(jnp.where(t == 0, 0, n_right + t), block).wait_recv()
        x_left_copy(nz + t, block).start()

    def gather_step(t, carry):
        block = slot(0, -t)
        z_right_copy(t - 1, block).wait_recv()

        @pl.when(t < n_right)
        def _():
            z_right_copy(t, block).start()

        x_right_copy(t, block).start()
        x_left_copy(t, block).start()

        @pl.when(t <= n_left)
        def _():
            above = slot(0, t)
            z_left_copy(t - 1, above).wait_recv()

            @pl.when(t < n_left)
            def _():
                z_left_copy(t, above).start()

            x_right_copy(n_right + t, above).start()
            x_left_copy(n_right + t, above).start()

        @pl.when(t > 1)
        def _():
            pass_right(t - 1)

        pass_left(t - 1)
        return carry

    lax.fori_loop(1, n_right + 1, gather_step, 0)
    pass_right(n_right)

    def finish(t, carry):
        x_right_copy(jnp.where(t == 0, 0, n_right + t), slot(-1, t)).wait_recv()
        x_left_copy(t + 1, slot(1, -t - 1)).wait_recv()
        x_right_copy(nz + t, slot(-2, -t - 1)).wait_recv()
        x_left_copy(nz + t, slot(2, t)).wait_recv()
        return carry

    lax.fori_loop(0, n_right, finish, 0)

    pair_copy = remote(
        pair_hbm.at[0], pair_out_hbm.at[0], p_send.at[0], p_recv.at[0], (d, s_next)
    )
    pair_copy.start()

    w_in.wait()
    wo_in.wait()
    member = lax.broadcasted_iota(jnp.int32, (n, HALF), 1) // dim
    for h in range(heads):
        v_sc[h * n : (h + 1) * n, HALF:] = jnp.where(member == h % (HALF // dim), 1.0, 0.0).astype(BF16)

    def out_copy(r):
        return pltpu.make_async_copy(x_sc.at[r], out_hbm.at[0, r], local_sem.at[3 + r])

    def row_step(r, carry):
        msa_copy(r).wait_recv()
        x_sc[r] = attend_row(
            x_sc[r],
            bias,
            w_sc,
            wo_sc[...],
            gain_ref[...],
            offset_ref[...],
            out_bias_ref[...],
            (q_sc, k_sc, v_sc, gate_sc, gated_sc),
            heads,
            dim,
        )
        out_copy(r).start()
        return carry

    lax.fori_loop(0, rows, row_step, 0)

    logit_copy.wait_send()
    gain_copy.wait_send()
    shard_copy(0, low, (d, s_next)).wait_send()
    shard_copy(1, low, (other, s_next)).wait_send()

    def drain_z_right(t, carry):
        z_right_copy(t, own).wait_send()
        return carry

    def drain_z_left(t, carry):
        z_left_copy(t, own).wait_send()
        return carry

    def drain_x(t, carry):
        x_right_copy(t, own).wait_send()
        x_left_copy(t, own).wait_send()
        return carry

    def drain_rows(r, carry):
        msa_copy(r).wait_send()
        out_copy(r).wait()
        return carry

    lax.fori_loop(0, n_right, drain_z_right, 0)
    lax.fori_loop(0, n_left, drain_z_left, 0)
    lax.fori_loop(0, nz + n_right, drain_x, 0)
    lax.fori_loop(0, rows, drain_rows, 0)
    pair_copy.wait()


NX, LOW = 4, 2


def body(
    ndap,
    ns,
    msa,
    pair,
    weights,
    w_out,
    logit,
    gain,
    pair_gain,
    offset,
    out_bias,
):
    _, rows, n, width = msa.shape
    pair_width, heads = logit.shape[1:]
    dim = width // heads
    nz = ndap // (NX * LOW)
    n_right, n_left = nz // 2, nz - 1 - nz // 2
    hops = nz + n_right
    hbm = pl.BlockSpec(memory_space=pltpu.HBM)
    vmem = pl.BlockSpec(memory_space=pltpu.VMEM)
    dma = pltpu.SemaphoreType.DMA
    return pl.pallas_call(
        functools.partial(kernel, NX, nz, ns, heads, dim),
        out_shape=(
            jax.ShapeDtypeStruct(msa.shape, F32),
            jax.ShapeDtypeStruct(pair.shape, F32),
        ),
        in_specs=[hbm] * 4 + [vmem] * 5,
        out_specs=(hbm, hbm),
        scratch_shapes=[
            pltpu.VMEM((rows, n, width), F32),
            pltpu.VMEM((rows, n, pair_width), F32),
            pltpu.VMEM((width, 4 * width), BF16),
            pltpu.VMEM((width, width), BF16),
            pltpu.VMEM((heads, pair_width), BF16),
            pltpu.VMEM((1, pair_width), F32),
            pltpu.VMEM((rows, heads * n), F32),
            pltpu.VMEM((2, rows, heads * n), F32),
            pltpu.VMEM((NX * nz, 2 * rows, heads * n), BF16),
            pltpu.VMEM((n, width), BF16),
            pltpu.VMEM((heads * n, HALF), BF16),
            pltpu.VMEM((heads * n, 2 * HALF), BF16),
            pltpu.VMEM((n, width), F32),
            pltpu.VMEM((n, width), BF16),
            dma((3 + rows,)),
            dma((2,)),
            dma((2,)),
            dma((2,)),
            dma((2,)),
            dma((n_right,)),
            dma((n_right,)),
            dma((n_left,)),
            dma((n_left,)),
            dma((hops,)),
            dma((hops,)),
            dma((hops,)),
            dma((hops,)),
            dma((rows,)),
            dma((rows,)),
            dma((1,)),
            dma((1,)),
        ],
        compiler_params=pltpu.CompilerParams(
            collective_id=0, has_side_effects=True, vmem_limit_bytes=48 << 20
        ),
    )(
        msa,
        pair,
        weights,
        w_out,
        logit[0].T,
        gain,
        pair_gain,
        offset,
        out_bias,
    )


def solution(mesh):
    wide = P("section", "dap", None, None)
    flat = P("section", None)
    in_specs = (wide, wide, P("section", None, None), P("section", None, None), P("section", None, None)) + (flat,) * 4
    return jax.shard_map(
        functools.partial(body, mesh.shape["dap"], mesh.shape["section"]),
        mesh=mesh,
        in_specs=in_specs,
        out_specs=(wide, wide),
        check_vma=False,
    )
```

time: 543 us -> 85.7 us (0.16)
  the two profiles are of different devices: /device:TPU:16 before, /device:TPU:40 now
where the time goes in v1:
time: 85.7 us; the launch traced here: 85.4 us
  Pallas kernels  74.8 us (87%)
  local copies, waits for them, and re-layouts  9.87 us (12%)
    pallas_call x1, Pallas kernels, body(): pl.pallas_call(functools.partial(kernel, NX, nz, ns, heads, dim), out_sha...  74.8 us
    unnamed x20, local copies, waits for them, and re-layouts  9.87 us

profile of v1, /device:TPU:40, one launch (start us, length us, event | category | flops | bytes accessed | tf_op | source)
XLA Modules:
  0.0 85.4 jit_solution(1460530283588244642)
XLA Ops:
  0.6 0.0 copy-start
  0.6 1.4 %copy-done = f32[1,4,384,256]{3,2,1,0:T(8,128)S(1)} copy-done((f32[1,4,384,256]{3,2,1,0:T(8,128)S(1)}, f32[1,4,384,256]{3,2,1,0:T(8,128)}, u32[]{:S(2)}) %copy-start) | copy-done | bytes 1572888
  2.0 0.0 copy-start.1
  2.0 1.1 %copy-done.1 = f32[1,4,384,128]{3,2,1,0:T(8,128)S(1)} copy-done((f32[1,4,384,128]{3,2,1,0:T(8,128)S(1)}, f32[1,4,384,128]{3,2,1,0:T(8,128)}, u32[]{:S(2)}) %copy-start.1) | copy-done | bytes 786456
  3.2 0.0 copy-start.2
  3.2 1.0 %copy-done.2 = bf16[1,256,1024]{2,1,0:T(8,128)(2,1)S(1)} copy-done((bf16[1,256,1024]{2,1,0:T(8,128)(2,1)S(1)}, bf16[1,256,1024]{2,1,0:T(8,128)(2,1)}, u32[]{:S(2)}) %copy-start.2) | copy-done | bytes 524312
  4.2 0.0 copy-start.3
  4.2 0.9 %copy-done.3 = bf16[1,256,256]{2,1,0:T(8,128)(2,1)S(1)} copy-done((bf16[1,256,256]{2,1,0:T(8,128)(2,1)S(1)}, bf16[1,256,256]{2,1,0:T(8,128)(2,1)}, u32[]{:S(2)}) %copy-start.3) | copy-done | bytes 131096
  5.1 0.0 copy-start.4
  5.1 0.7 copy-done.4
  5.8 0.0 copy-start.5
  5.8 0.7 copy-done.5
  6.5 0.0 copy-start.6
  6.5 0.7 copy-done.6
  7.2 0.0 copy-start.7
  7.2 0.7 copy-done.7
  7.8 0.0 copy-start.8
  7.8 0.7 copy-done.8
  8.5 74.8 %shard_map.104 = (f32[1,4,384,256]{3,2,1,0:T(8,128)S(1)}, f32[1,4,384,128]{3,2,1,0:T(8,128)S(1)}) custom-call(f32[1,4,384,256]{3,2,1,0:T(8,128)S(1)} %copy-done, f32[1,4,384,128]{3,2,1,0:T(8,128)S(1)} %copy-done.1, bf16[1,256,1024]{2,1,0:T(8,128)(2,1)S(1)} %copy-done.2, bf16[1,256,256]{2,1,0:T(8,128)(2,1)S(1)} %copy-done.3, bf16[8,128]{1,0:T(8,128)(2,1)S(1)} %bitcast.3, ...), custom_call_target="tpu_custom_call" | custom-call | tf_op jit(solution)/shard_map/pallas_call | solution.py:365
  83.3 1.1 %copy.13 = f32[1,4,384,256]{3,2,1,0:T(8,128)} copy(f32[1,4,384,256]{3,2,1,0:T(8,128)S(1)} %get-tuple-element.4) | data formatting | bytes 3145728
  84.5 0.9 %copy.14 = f32[1,4,384,128]{3,2,1,0:T(8,128)} copy(f32[1,4,384,128]{3,2,1,0:T(8,128)S(1)} %get-tuple-element.5) | data formatting | bytes 1572864
Async XLA Ops:
  0.6 1.4 %copy-start = (f32[1,4,384,256]{3,2,1,0:T(8,128)S(1)}, f32[1,4,384,256]{3,2,1,0:T(8,128)}, u32[]{:S(2)}) copy-start(f32[1,4,384,256]{3,2,1,0:T(8,128)} %msa_hbm.1) | copy-start | bytes 4718596
  2.0 1.1 %copy-start.1 = (f32[1,4,384,128]{3,2,1,0:T(8,128)S(1)}, f32[1,4,384,128]{3,2,1,0:T(8,128)}, u32[]{:S(2)}) copy-start(f32[1,4,384,128]{3,2,1,0:T(8,128)} %pair_hbm.1) | copy-start | bytes 2359300
  3.2 1.0 %copy-start.2 = (bf16[1,256,1024]{2,1,0:T(8,128)(2,1)S(1)}, bf16[1,256,1024]{2,1,0:T(8,128)(2,1)}, u32[]{:S(2)}) copy-start(bf16[1,256,1024]{2,1,0:T(8,128)(2,1)} %weights_hbm.1) | copy-start | bytes 1572868
  4.2 0.9 %copy-start.3 = (bf16[1,256,256]{2,1,0:T(8,128)(2,1)S(1)}, bf16[1,256,256]{2,1,0:T(8,128)(2,1)}, u32[]{:S(2)}) copy-start(bf16[1,256,256]{2,1,0:T(8,128)(2,1)} %w_out_hbm.1) | copy-start | bytes 393220
  5.1 0.7 copy-start.4
  5.8 0.7 copy-start.5
  6.5 0.7 copy-start.6
  7.2 0.7 copy-start.7
  7.8 0.7 copy-start.8

commit v2 on v1

--- a/solution.py
+++ b/solution.py
@@ -14,17 +14,16 @@
 HALF = 128
 
 
-def standardize(values, gain):
+def whiten(values):
     center = values - jnp.mean(values, axis=-1, keepdims=True)
     spread = jnp.mean(center * center, axis=-1, keepdims=True)
-    return center * lax.rsqrt(spread + EPSILON) * gain
-
-
-def attend_row(x, bias, weights, w_out, gain, offset, out_bias, scratch, heads, dim):
-    q_sc, k_sc, v_sc, gate_sc, gated_sc = scratch
+    return center * lax.rsqrt(spread + EPSILON)
+
+
+def prepare_row(r, x, weights, gain, offset, q_sc, k_sc, v_sc, gate_sc, heads, dim):
     n, width = x.shape
     per_half = HALF // dim
-    normed = standardize(x, gain).astype(BF16)
+    normed = (whiten(x) * gain).astype(BF16)
     member = lax.broadcasted_iota(jnp.int32, (n, HALF), 1) // dim
 
     def project(block):
@@ -32,24 +31,29 @@
             normed, weights[:, block * width : (block + 1) * width], preferred_element_type=F32
         )
 
-    q_sc[...] = (project(0) * (1.0 / dim**0.5)).astype(BF16)
+    q_sc[r] = (project(0) * (1.0 / dim**0.5)).astype(BF16)
     keys = project(1)
     values = project(2)
     for h in range(heads):
         lanes = slice(h // per_half * HALF, (h // per_half + 1) * HALF)
         mine = member == h % per_half
-        k_sc[h * n : (h + 1) * n, :] = jnp.where(mine, keys[:, lanes], 0.0).astype(BF16)
-        v_sc[h * n : (h + 1) * n, :HALF] = jnp.where(mine, values[:, lanes], 0.0).astype(BF16)
-    gate_sc[...] = jax.nn.sigmoid(project(3) + offset)
+        k_sc[r, h * n : (h + 1) * n, :] = jnp.where(mine, keys[:, lanes], 0.0).astype(BF16)
+        v_sc[r, h * n : (h + 1) * n, :HALF] = jnp.where(mine, values[:, lanes], 0.0).astype(BF16)
+    gate_sc[r] = jax.nn.sigmoid(project(3) + offset)
+
+
+def attend_row(r, x, bias, w_out, out_bias, q_sc, k_sc, v_sc, gate_sc, gated_sc, heads, dim):
+    n, width = x.shape
+    per_half = HALF // dim
     for half in range(width // HALF):
         lanes = slice(half * HALF, (half + 1) * HALF)
-        queries = q_sc[:, lanes]
+        queries = q_sc[r, :, lanes]
         total = None
         for pair in range(per_half // 2):
             h = half * per_half + pair * 2
             scores = lax.dot_general(
                 queries,
-                k_sc[h * n : (h + 2) * n, :],
+                k_sc[r, h * n : (h + 2) * n, :],
                 (((1,), (1,)), ((), ())),
                 preferred_element_type=F32,
             )
@@ -61,11 +65,11 @@
                 probs.append(jnp.exp(shifted - top).astype(BF16))
             part = jnp.dot(
                 jnp.concatenate(probs, axis=-1),
-                v_sc[h * n : (h + 2) * n, :],
+                v_sc[r, h * n : (h + 2) * n, :],
                 preferred_element_type=F32,
             )
             total = part if total is None else total + part
-        gated_sc[:, lanes] = (total[:, :HALF] / total[:, HALF:] * gate_sc[:, lanes]).astype(BF16)
+        gated_sc[:, lanes] = (total[:, :HALF] / total[:, HALF:] * gate_sc[r, :, lanes]).astype(BF16)
     return x + (jnp.dot(gated_sc[...], w_out, preferred_element_type=F32) + out_bias)
 
 
@@ -79,21 +83,25 @@
     pair_hbm,
     weights_hbm,
     w_out_hbm,
-    logit_ref,
-    gain_ref,
-    pair_gain_ref,
-    offset_ref,
-    out_bias_ref,
+    logit_hbm,
+    gain_hbm,
+    pair_gain_hbm,
+    offset_hbm,
+    out_bias_hbm,
     out_hbm,
     pair_out_hbm,
     x_sc,
     pair_sc,
     w_sc,
     wo_sc,
+    gain_sc,
+    offset_sc,
+    out_bias_sc,
     next_logit,
     next_gain,
     shard,
     stage,
+    relay,
     bias,
     q_sc,
     k_sc,
@@ -117,6 +125,9 @@
     m_recv,
     p_send,
     p_recv,
+    leg_send,
+    leg_recv,
+    pass_send,
 ):
     rows, n = x_sc.shape[0], x_sc.shape[1]
     n_right = nz // 2
@@ -135,16 +146,37 @@
     other = d + 1 - 2 * low
     s_next = lax.rem(s + 1, ns)
     s_prev = lax.rem(s + ns - 1, ns)
+    core = lax.rem(s, 2)
+    y = 2 * lax.div(s, 2) + low
+    y_back = lax.rem(y + ns - 3, ns)
+    y_ahead = lax.rem(y + 3, ns)
+
+    def chip(at, on_core):
+        return (d - low + lax.rem(at, 2), 2 * lax.div(at, 2) + on_core)
+
+    relay_to = chip(y_back, 1)
+    relay_from = chip(y_ahead, 1)
+    last_stop = chip(y_back, 0)
 
     def slot(dx, dz):
         return lax.rem(x + dx + nx, nx) * nz + lax.rem(z + dz + nz, nz)
 
-    pair_in = pltpu.make_async_copy(pair_hbm.at[0], pair_sc, local_sem.at[0])
-    w_in = pltpu.make_async_copy(weights_hbm.at[0], w_sc, local_sem.at[1])
-    wo_in = pltpu.make_async_copy(w_out_hbm.at[0], wo_sc, local_sem.at[2])
+    pair_in = pltpu.make_async_copy(pair_hbm.at[0], pair_sc, local_sem.at[rows])
+    fetched = [
+        pltpu.make_async_copy(src, dst, local_sem.at[rows + 1 + i])
+        for i, (src, dst) in enumerate(
+            (
+                (weights_hbm.at[0], w_sc),
+                (w_out_hbm.at[0], wo_sc),
+                (gain_hbm, gain_sc),
+                (offset_hbm, offset_sc),
+                (out_bias_hbm, out_bias_sc),
+            )
+        )
+    ]
     pair_in.start()
-    w_in.start()
-    wo_in.start()
+    for copy in fetched:
+        copy.start()
 
     barrier = pltpu.get_barrier_semaphore()
     peers = (
@@ -156,10 +188,17 @@
         (d, s_prev),
         (other, s_next),
         (other, s_prev),
+        relay_from,
     )
     for peer in peers:
         pl.semaphore_signal(barrier, inc=1, device_id=peer, device_id_type=MESH)
-    pl.semaphore_wait(barrier, len(peers))
+
+    @pl.when(core == 1)
+    def _():
+        pl.semaphore_signal(barrier, inc=1, device_id=relay_to, device_id_type=MESH)
+        pl.semaphore_signal(barrier, inc=1, device_id=last_stop, device_id_type=MESH)
+
+    pl.semaphore_wait(barrier, len(peers) + 2 * core)
 
     def remote(src, dst, send, recv, peer):
         return pltpu.make_async_remote_copy(
@@ -171,22 +210,60 @@
             device_id_type=MESH,
         )
 
-    logit_copy = remote(logit_ref, next_logit, w_send.at[0], w_recv.at[0], (d, s_prev))
-    gain_copy = remote(pair_gain_ref, next_gain, w_send.at[1], w_recv.at[1], (d, s_prev))
+    logit_copy = remote(logit_hbm, next_logit, w_send.at[0], w_recv.at[0], (d, s_prev))
+    gain_copy = remote(pair_gain_hbm, next_gain, w_send.at[1], w_recv.at[1], (d, s_prev))
     logit_copy.start()
     gain_copy.start()
 
     def msa_copy(r):
         return remote(msa_hbm.at[0, r], x_sc.at[r], m_send.at[r], m_recv.at[r], (d, s_next))
 
+    def pair_copy(r):
+        return remote(
+            pair_hbm.at[0, r], pair_out_hbm.at[0, r], p_send.at[r], p_recv.at[r], (d, s_next)
+        )
+
+    def leg_copy(k):
+        return remote(
+            pair_hbm.at[0, k + 1], relay.at[k], leg_send.at[k], leg_recv.at[k], relay_to
+        )
+
+    def pass_copy(k):
+        return remote(
+            relay.at[k], pair_out_hbm.at[0, k + 1], pass_send.at[k], p_recv.at[k + 1], last_stop
+        )
+
+    def relay_step(k):
+        @pl.when(core == 1)
+        def _():
+            leg_copy(k).wait_recv()
+            pass_copy(k).start()
+            if k + 1 < rows - 1:
+                leg_copy(k + 1).start()
+
     msa_copy(0).start()
 
+    @pl.when(core == 1)
+    def _():
+        leg_copy(0).start()
+
+    member = lax.broadcasted_iota(jnp.int32, (n, HALF), 1) // dim
+
+    def ones_step(r, carry):
+        for h in range(heads):
+            mine = member == h % (HALF // dim)
+            v_sc[r, h * n : (h + 1) * n, HALF:] = jnp.where(mine, 1.0, 0.0).astype(BF16)
+        return carry
+
+    lax.fori_loop(0, rows, ones_step, 0)
     pair_in.wait()
+    for r in range(rows):
+        pair_sc[r] = whiten(pair_sc[r])
     logit_copy.wait_recv()
     gain_copy.wait_recv()
     logits = next_logit[...]
     for r in range(rows):
-        normed = standardize(pair_sc[r], next_gain[...]).astype(BF16)
+        normed = (pair_sc[r] * next_gain[...]).astype(BF16)
         shard_row = lax.dot_general(
             logits, normed, (((1,), (1,)), ((), ())), preferred_element_type=F32
         )
@@ -198,11 +275,19 @@
 
     shard_copy(0, low, (d, s_next)).start()
     shard_copy(1, low, (other, s_next)).start()
-    for r in range(1, rows):
-        msa_copy(r).start()
+    msa_copy(1).start()
+
+    @pl.when(core == 0)
+    def _():
+        for r in range(2, rows):
+            msa_copy(r).start()
+        for r in range(rows):
+            pair_copy(r).start()
+
     shard_copy(0, 0, (d, s_next)).wait_recv()
     shard_copy(1, 1, (other, s_next)).wait_recv()
-    bias[slot(0, 0)] = jnp.concatenate([stage[0], stage[1]], axis=0).astype(BF16)
+    own = slot(0, 0)
+    bias[own] = jnp.concatenate([stage[0], stage[1]], axis=0).astype(BF16)
 
     def z_right_copy(t, block):
         return remote(bias.at[block], bias.at[block], zr_send.at[t], zr_recv.at[t], (z_right, s))
@@ -216,11 +301,11 @@
     def x_left_copy(t, block):
         return remote(bias.at[block], bias.at[block], xl_send.at[t], xl_recv.at[t], (x_left, s))
 
-    own = slot(0, 0)
     z_right_copy(0, own).start()
     z_left_copy(0, own).start()
     x_right_copy(0, own).start()
     x_left_copy(0, own).start()
+    relay_step(0)
 
     def pass_right(t):
         block = slot(-1, -t)
@@ -260,10 +345,38 @@
             pass_right(t - 1)
 
         pass_left(t - 1)
+        for r in range(2, rows):
+
+            @pl.when((t == 3 * r - 4) & (core == 1))
+            def _(r=r):
+                msa_copy(r - 2).wait_send()
+                msa_copy(r).start()
+
+        @pl.when(t == 4)
+        def _():
+            relay_step(1)
+
         return carry
 
     lax.fori_loop(1, n_right + 1, gather_step, 0)
     pass_right(n_right)
+    relay_step(2)
+
+    @pl.when(core == 1)
+    def _():
+        pair_copy(0).start()
+
+    for copy in fetched:
+        copy.wait()
+
+    def prepare(r, carry):
+        msa_copy(r).wait_recv()
+        prepare_row(
+            r, x_sc[r], w_sc, gain_sc[...], offset_sc[...], q_sc, k_sc, v_sc, gate_sc, heads, dim
+        )
+        return carry
+
+    lax.fori_loop(0, rows - 1, prepare, 0)
 
     def finish(t, carry):
         x_right_copy(jnp.where(t == 0, 0, n_right + t), slot(-1, t)).wait_recv()
@@ -274,31 +387,25 @@
 
     lax.fori_loop(0, n_right, finish, 0)
 
-    pair_copy = remote(
-        pair_hbm.at[0], pair_out_hbm.at[0], p_send.at[0], p_recv.at[0], (d, s_next)
-    )
-    pair_copy.start()
-
-    w_in.wait()
-    wo_in.wait()
-    member = lax.broadcasted_iota(jnp.int32, (n, HALF), 1) // dim
-    for h in range(heads):
-        v_sc[h * n : (h + 1) * n, HALF:] = jnp.where(member == h % (HALF // dim), 1.0, 0.0).astype(BF16)
-
     def out_copy(r):
-        return pltpu.make_async_copy(x_sc.at[r], out_hbm.at[0, r], local_sem.at[3 + r])
+        return pltpu.make_async_copy(x_sc.at[r], out_hbm.at[0, r], local_sem.at[r])
 
     def row_step(r, carry):
-        msa_copy(r).wait_recv()
+        @pl.when(r == rows - 1)
+        def _():
+            prepare(r, 0)
+
         x_sc[r] = attend_row(
+            r,
             x_sc[r],
             bias,
-            w_sc,
             wo_sc[...],
-            gain_ref[...],
-            offset_ref[...],
-            out_bias_ref[...],
-            (q_sc, k_sc, v_sc, gate_sc, gated_sc),
+            out_bias_sc[...],
+            q_sc,
+            k_sc,
+            v_sc,
+            gate_sc,
+            gated_sc,
             heads,
             dim,
         )
@@ -326,7 +433,10 @@
         return carry
 
     def drain_rows(r, carry):
-        msa_copy(r).wait_send()
+        @pl.when((core == 0) | (r >= rows - 2))
+        def _():
+            msa_copy(r).wait_send()
+
         out_copy(r).wait()
         return carry
 
@@ -334,7 +444,20 @@
     lax.fori_loop(0, n_left, drain_z_left, 0)
     lax.fori_loop(0, nz + n_right, drain_x, 0)
     lax.fori_loop(0, rows, drain_rows, 0)
-    pair_copy.wait()
+    pair_copy(0).wait_send()
+    for k in range(rows - 1):
+
+        @pl.when(core == 1)
+        def _(k=k):
+            leg_copy(k).wait_send()
+            pass_copy(k).wait_send()
+
+        @pl.when(core == 0)
+        def _(k=k):
+            pair_copy(k + 1).wait_send()
+
+    for r in range(rows):
+        pair_copy(r).wait_recv()
 
 
 NX, LOW = 4, 2
@@ -360,7 +483,6 @@
     n_right, n_left = nz // 2, nz - 1 - nz // 2
     hops = nz + n_right
     hbm = pl.BlockSpec(memory_space=pltpu.HBM)
-    vmem = pl.BlockSpec(memory_space=pltpu.VMEM)
     dma = pltpu.SemaphoreType.DMA
     return pl.pallas_call(
         functools.partial(kernel, NX, nz, ns, heads, dim),
@@ -368,24 +490,28 @@
             jax.ShapeDtypeStruct(msa.shape, F32),
             jax.ShapeDtypeStruct(pair.shape, F32),
         ),
-        in_specs=[hbm] * 4 + [vmem] * 5,
+        in_specs=[hbm] * 9,
         out_specs=(hbm, hbm),
         scratch_shapes=[
             pltpu.VMEM((rows, n, width), F32),
             pltpu.VMEM((rows, n, pair_width), F32),
             pltpu.VMEM((width, 4 * width), BF16),
             pltpu.VMEM((width, width), BF16),
+            pltpu.VMEM((1, width), F32),
+            pltpu.VMEM((1, width), F32),
+            pltpu.VMEM((1, width), F32),
             pltpu.VMEM((heads, pair_width), BF16),
             pltpu.VMEM((1, pair_width), F32),
             pltpu.VMEM((rows, heads * n), F32),
             pltpu.VMEM((2, rows, heads * n), F32),
+            pltpu.VMEM((rows - 1, n, pair_width), F32),
             pltpu.VMEM((NX * nz, 2 * rows, heads * n), BF16),
+            pltpu.VMEM((rows, n, width), BF16),
+            pltpu.VMEM((rows, heads * n, HALF), BF16),
+            pltpu.VMEM((rows, heads * n, 2 * HALF), BF16),
+            pltpu.VMEM((rows, n, width), F32),
             pltpu.VMEM((n, width), BF16),
-            pltpu.VMEM((heads * n, HALF), BF16),
-            pltpu.VMEM((heads * n, 2 * HALF), BF16),
-            pltpu.VMEM((n, width), F32),
-            pltpu.VMEM((n, width), BF16),
-            dma((3 + rows,)),
+            dma((rows + 6,)),
             dma((2,)),
             dma((2,)),
             dma((2,)),
@@ -400,11 +526,14 @@
             dma((hops,)),
             dma((rows,)),
             dma((rows,)),
-            dma((1,)),
-            dma((1,)),
+            dma((rows,)),
+            dma((rows,)),
+            dma((rows - 1,)),
+            dma((rows - 1,)),
+            dma((rows - 1,)),
         ],
         compiler_params=pltpu.CompilerParams(
-            collective_id=0, has_side_effects=True, vmem_limit_bytes=48 << 20
+            collective_id=0, has_side_effects=True, vmem_limit_bytes=60 << 20
         ),
     )(
         msa,
@@ -421,12 +550,12 @@
 
 def solution(mesh):
     wide = P("section", "dap", None, None)
+    deep = P("section", None, None)
     flat = P("section", None)
-    in_specs = (wide, wide, P("section", None, None), P("section", None, None), P("section", None, None)) + (flat,) * 4
     return jax.shard_map(
         functools.partial(body, mesh.shape["dap"], mesh.shape["section"]),
         mesh=mesh,
-        in_specs=in_specs,
+        in_specs=(wide, wide, deep, deep, deep, flat, flat, flat, flat),
         out_specs=(wide, wide),
         check_vma=False,
     )

time: 85.7 us -> 76.5 us (0.89)
  local copies, waits for them, and re-layouts: 9.87 us -> 3.61 us
  Pallas kernels: 74.8 us -> 72.1 us
    unnamed x20 -> x4, local copies, waits for them, and re-layouts: 9.87 us -> 3.61 us
    pallas_call x1, Pallas kernels: 74.8 us -> 72.1 us  [body(): pl.pallas_call(functools.partial(kernel, NX, nz, ns, heads, dim), out_sha...]
where the time goes in v2:
time: 76.5 us; the launch traced here: 76.3 us
  Pallas kernels  72.1 us (94%)
  local copies, waits for them, and re-layouts  3.61 us (5%)
    pallas_call x1, Pallas kernels, body(): pl.pallas_call(functools.partial(kernel, NX, nz, ns, heads, dim), out_sha...  72.1 us
    unnamed x4, local copies, waits for them, and re-layouts  3.61 us

profile of v2, /device:TPU:40, one launch (start us, length us, event | category | flops | bytes accessed | tf_op | source)
XLA Modules:
  0.0 76.3 jit_solution(598434248172875744)
XLA Ops:
  0.6 72.1 %shard_map.104 = (f32[1,4,384,256]{3,2,1,0:T(8,128)}, f32[1,4,384,128]{3,2,1,0:T(8,128)}) custom-call(f32[1,4,384,256]{3,2,1,0:T(8,128)} %msa_hbm.1, f32[1,4,384,128]{3,2,1,0:T(8,128)} %pair_hbm.1, bf16[1,256,1024]{2,1,0:T(8,128)(2,1)} %weights_hbm.1, bf16[1,256,256]{2,1,0:T(8,128)(2,1)} %w_out_hbm.1, bf16[8,128]{1,0:T(8,128)(2,1)} %bitcast.3, ...), custom_call_target="tpu_custom_call" | custom-call | tf_op jit(solution)/shard_map/pallas_call | solution.py:487
  72.7 0.0 copy-start
  72.7 2.7 %copy.13 = f32[1,4,384,256]{3,2,1,0:T(8,128)} copy(f32[1,4,384,256]{3,2,1,0:T(8,128)} %get-tuple-element.4) | data formatting | bytes 3145728
  75.5 0.0 copy-done
  75.5 0.9 %copy.14 = f32[1,4,384,128]{3,2,1,0:T(8,128)} copy(f32[1,4,384,128]{3,2,1,0:T(8,128)S(1)} %copy-done) | data formatting | bytes 1572864
Async XLA Ops:
  72.7 2.7 %copy-start = (f32[1,4,384,128]{3,2,1,0:T(8,128)S(1)}, f32[1,4,384,128]{3,2,1,0:T(8,128)}, u32[]{:S(2)}) copy-start(f32[1,4,384,128]{3,2,1,0:T(8,128)} %get-tuple-element.5) | copy-start | bytes 2359300

commit v3 on v2

--- a/solution.py
+++ b/solution.py
@@ -100,6 +100,7 @@
     next_logit,
     next_gain,
     shard,
+    shard_half,
     stage,
     relay,
     bias,
@@ -121,6 +122,12 @@
     xr_recv,
     xl_send,
     xl_recv,
+    far_send,
+    far_recv,
+    fr_send,
+    fr_recv,
+    fl_send,
+    fl_recv,
     m_send,
     m_recv,
     p_send,
@@ -143,6 +150,7 @@
     z_left = base + 2 * lax.rem(z + nz - 1, nz)
     x_right = lax.rem(d + 2 * nz, ndap)
     x_left = lax.rem(d + ndap - 2 * nz, ndap)
+    x_far = lax.rem(d + 4 * nz, ndap)
     other = d + 1 - 2 * low
     s_next = lax.rem(s + 1, ns)
     s_prev = lax.rem(s + ns - 1, ns)
@@ -184,6 +192,7 @@
         (z_left, s),
         (x_right, s),
         (x_left, s),
+        (x_far, s),
         (d, s_next),
         (d, s_prev),
         (other, s_next),
@@ -218,6 +227,16 @@
     def msa_copy(r):
         return remote(msa_hbm.at[0, r], x_sc.at[r], m_send.at[r], m_recv.at[r], (d, s_next))
 
+    def head_copy(half):
+        part = pl.ds(half * (n // 2), n // 2)
+        return remote(
+            msa_hbm.at[0, 0, part],
+            x_sc.at[0, part],
+            m_send.at[half * rows],
+            m_recv.at[half * rows],
+            (d, s_next),
+        )
+
     def pair_copy(r):
         return remote(
             pair_hbm.at[0, r], pair_out_hbm.at[0, r], p_send.at[r], p_recv.at[r], (d, s_next)
@@ -238,15 +257,10 @@
         def _():
             leg_copy(k).wait_recv()
             pass_copy(k).start()
-            if k + 1 < rows - 1:
-                leg_copy(k + 1).start()
-
-    msa_copy(0).start()
-
-    @pl.when(core == 1)
-    def _():
-        leg_copy(0).start()
-
+            if k + 2 < rows - 1:
+                leg_copy(k + 2).start()
+
+    head_copy(0).start()
     member = lax.broadcasted_iota(jnp.int32, (n, HALF), 1) // dim
 
     def ones_step(r, carry):
@@ -261,6 +275,12 @@
         pair_sc[r] = whiten(pair_sc[r])
     logit_copy.wait_recv()
     gain_copy.wait_recv()
+
+    @pl.when(core == 1)
+    def _():
+        leg_copy(0).start()
+        leg_copy(1).start()
+
     logits = next_logit[...]
     for r in range(rows):
         normed = (pair_sc[r] * next_gain[...]).astype(BF16)
@@ -270,52 +290,74 @@
         for h in range(heads):
             shard[r : r + 1, h * n : (h + 1) * n] = shard_row[h : h + 1, :]
 
+    shard_half[...] = shard[...].astype(BF16)
+
     def shard_copy(index, row, peer):
-        return remote(shard, stage.at[row], b_send.at[index], b_recv.at[row], peer)
+        return remote(shard_half, stage.at[row], b_send.at[index], b_recv.at[row], peer)
 
     shard_copy(0, low, (d, s_next)).start()
     shard_copy(1, low, (other, s_next)).start()
+    head_copy(1).start()
     msa_copy(1).start()
+    msa_copy(2).start()
 
     @pl.when(core == 0)
     def _():
-        for r in range(2, rows):
-            msa_copy(r).start()
+        msa_copy(3).start()
         for r in range(rows):
             pair_copy(r).start()
 
     shard_copy(0, 0, (d, s_next)).wait_recv()
     shard_copy(1, 1, (other, s_next)).wait_recv()
     own = slot(0, 0)
-    bias[own] = jnp.concatenate([stage[0], stage[1]], axis=0).astype(BF16)
+    bias[own] = jnp.concatenate([stage[0].astype(F32), stage[1].astype(F32)], axis=0).astype(BF16)
+
+    def block_copy(send, recv, t, block, peer):
+        return remote(bias.at[block], bias.at[block], send.at[t], recv.at[t], (peer, s))
 
     def z_right_copy(t, block):
-        return remote(bias.at[block], bias.at[block], zr_send.at[t], zr_recv.at[t], (z_right, s))
+        return block_copy(zr_send, zr_recv, t, block, z_right)
 
     def z_left_copy(t, block):
-        return remote(bias.at[block], bias.at[block], zl_send.at[t], zl_recv.at[t], (z_left, s))
+        return block_copy(zl_send, zl_recv, t, block, z_left)
 
     def x_right_copy(t, block):
-        return remote(bias.at[block], bias.at[block], xr_send.at[t], xr_recv.at[t], (x_right, s))
+        return block_copy(xr_send, xr_recv, t, block, x_right)
 
     def x_left_copy(t, block):
-        return remote(bias.at[block], bias.at[block], xl_send.at[t], xl_recv.at[t], (x_left, s))
-
+        return block_copy(xl_send, xl_recv, t, block, x_left)
+
+    def far_copy(block):
+        return block_copy(far_send, far_recv, 0, block, x_far)
+
+    def far_right_copy(t, block):
+        return block_copy(fr_send, fr_recv, t, block, z_right)
+
+    def far_left_copy(t, block):
+        return block_copy(fl_send, fl_recv, t, block, z_left)
+
+    far_copy(own).start()
     z_right_copy(0, own).start()
     z_left_copy(0, own).start()
     x_right_copy(0, own).start()
     x_left_copy(0, own).start()
-    relay_step(0)
-
-    def pass_right(t):
-        block = slot(-1, -t)
-        x_right_copy(t, block).wait_recv()
-        x_right_copy(nz + t - 1, block).start()
-
-    def pass_left(t):
-        block = slot(1, t)
-        x_left_copy(jnp.where(t == 0, 0, n_right + t), block).wait_recv()
-        x_left_copy(nz + t, block).start()
+
+    def far_step(t):
+        below = slot(2, -t)
+        far_right_copy(t - 1, below).wait_recv()
+
+        @pl.when(t < n_right)
+        def _():
+            far_right_copy(t, below).start()
+
+        @pl.when(t <= n_left)
+        def _():
+            above = slot(2, t)
+            far_left_copy(t - 1, above).wait_recv()
+
+            @pl.when(t < n_left)
+            def _():
+                far_left_copy(t, above).start()
 
     def gather_step(t, carry):
         block = slot(0, -t)
@@ -340,17 +382,24 @@
             x_right_copy(n_right + t, above).start()
             x_left_copy(n_right + t, above).start()
 
+        @pl.when(t == 1)
+        def _():
+            far = slot(2, 0)
+            far_copy(far).wait_recv()
+            far_right_copy(0, far).start()
+            far_left_copy(0, far).start()
+
         @pl.when(t > 1)
         def _():
-            pass_right(t - 1)
-
-        pass_left(t - 1)
-        for r in range(2, rows):
-
-            @pl.when((t == 3 * r - 4) & (core == 1))
-            def _(r=r):
-                msa_copy(r - 2).wait_send()
-                msa_copy(r).start()
+            far_step(t - 1)
+
+        @pl.when(t == 1)
+        def _():
+            relay_step(0)
+
+        @pl.when((t == 2) & (core == 1))
+        def _():
+            msa_copy(3).start()
 
         @pl.when(t == 4)
         def _():
@@ -359,7 +408,7 @@
         return carry
 
     lax.fori_loop(1, n_right + 1, gather_step, 0)
-    pass_right(n_right)
+    far_step(n_right)
     relay_step(2)
 
     @pl.when(core == 1)
@@ -370,7 +419,15 @@
         copy.wait()
 
     def prepare(r, carry):
-        msa_copy(r).wait_recv()
+        @pl.when(r == 0)
+        def _():
+            head_copy(0).wait_recv()
+            head_copy(1).wait_recv()
+
+        @pl.when(r > 0)
+        def _():
+            msa_copy(r).wait_recv()
+
         prepare_row(
             r, x_sc[r], w_sc, gain_sc[...], offset_sc[...], q_sc, k_sc, v_sc, gate_sc, heads, dim
         )
@@ -379,13 +436,12 @@
     lax.fori_loop(0, rows - 1, prepare, 0)
 
     def finish(t, carry):
-        x_right_copy(jnp.where(t == 0, 0, n_right + t), slot(-1, t)).wait_recv()
-        x_left_copy(t + 1, slot(1, -t - 1)).wait_recv()
-        x_right_copy(nz + t, slot(-2, -t - 1)).wait_recv()
-        x_left_copy(nz + t, slot(2, t)).wait_recv()
-        return carry
-
-    lax.fori_loop(0, n_right, finish, 0)
+        below, above = jnp.where(t > n_right, 0, t), jnp.where(t > n_right, t - n_right, 0)
+        x_right_copy(t, slot(-1, above - below)).wait_recv()
+        x_left_copy(t, slot(1, above - below)).wait_recv()
+        return carry
+
+    lax.fori_loop(0, nz, finish, 0)
 
     def out_copy(r):
         return pltpu.make_async_copy(x_sc.at[r], out_hbm.at[0, r], local_sem.at[r])
@@ -421,10 +477,12 @@
 
     def drain_z_right(t, carry):
         z_right_copy(t, own).wait_send()
+        far_right_copy(t, own).wait_send()
         return carry
 
     def drain_z_left(t, carry):
         z_left_copy(t, own).wait_send()
+        far_left_copy(t, own).wait_send()
         return carry
 
     def drain_x(t, carry):
@@ -433,7 +491,7 @@
         return carry
 
     def drain_rows(r, carry):
-        @pl.when((core == 0) | (r >= rows - 2))
+        @pl.when(r > 0)
         def _():
             msa_copy(r).wait_send()
 
@@ -442,8 +500,11 @@
 
     lax.fori_loop(0, n_right, drain_z_right, 0)
     lax.fori_loop(0, n_left, drain_z_left, 0)
-    lax.fori_loop(0, nz + n_right, drain_x, 0)
+    lax.fori_loop(0, nz, drain_x, 0)
+    far_copy(own).wait_send()
     lax.fori_loop(0, rows, drain_rows, 0)
+    head_copy(0).wait_send()
+    head_copy(1).wait_send()
     pair_copy(0).wait_send()
     for k in range(rows - 1):
 
@@ -481,9 +542,9 @@
     dim = width // heads
     nz = ndap // (NX * LOW)
     n_right, n_left = nz // 2, nz - 1 - nz // 2
-    hops = nz + n_right
     hbm = pl.BlockSpec(memory_space=pltpu.HBM)
     dma = pltpu.SemaphoreType.DMA
+    operands = (msa, pair, weights, w_out, logit[0].T, gain, pair_gain, offset, out_bias)
     return pl.pallas_call(
         functools.partial(kernel, NX, nz, ns, heads, dim),
         out_shape=(
@@ -503,7 +564,8 @@
             pltpu.VMEM((heads, pair_width), BF16),
             pltpu.VMEM((1, pair_width), F32),
             pltpu.VMEM((rows, heads * n), F32),
-            pltpu.VMEM((2, rows, heads * n), F32),
+            pltpu.VMEM((rows, heads * n), BF16),
+            pltpu.VMEM((2, rows, heads * n), BF16),
             pltpu.VMEM((rows - 1, n, pair_width), F32),
             pltpu.VMEM((NX * nz, 2 * rows, heads * n), BF16),
             pltpu.VMEM((rows, n, width), BF16),
@@ -520,12 +582,18 @@
             dma((n_right,)),
             dma((n_left,)),
             dma((n_left,)),
-            dma((hops,)),
-            dma((hops,)),
-            dma((hops,)),
-            dma((hops,)),
-            dma((rows,)),
-            dma((rows,)),
+            dma((nz,)),
+            dma((nz,)),
+            dma((nz,)),
+            dma((nz,)),
+            dma((1,)),
+            dma((1,)),
+            dma((n_right,)),
+            dma((n_right,)),
+            dma((n_left,)),
+            dma((n_left,)),
+            dma((rows + 1,)),
+            dma((rows + 1,)),
             dma((rows,)),
             dma((rows,)),
             dma((rows - 1,)),
@@ -533,19 +601,9 @@
             dma((rows - 1,)),
         ],
         compiler_params=pltpu.CompilerParams(
-            collective_id=0, has_side_effects=True, vmem_limit_bytes=60 << 20
+            collective_id=0, has_side_effects=True, vmem_limit_bytes=44 << 20
         ),
-    )(
-        msa,
-        pair,
-        weights,
-        w_out,
-        logit[0].T,
-        gain,
-        pair_gain,
-        offset,
-        out_bias,
-    )
+    )(*(pltpu.with_memory_space_constraint(operand, pltpu.HBM) for operand in operands))
 
 
 def solution(mesh):

time: 76.5 us -> 69.4 us (0.907)
  the two profiles are of different devices: /device:TPU:40 before, /device:TPU:8 now
where the time goes in v3:
time: 69.4 us; the launch traced here: 69.3 us
  Pallas kernels  66.6 us (96%)
  local copies, waits for them, and re-layouts  2.02 us (3%)
    pallas_call x1, Pallas kernels, body(): pl.pallas_call(functools.partial(kernel, NX, nz, ns, heads, dim), out_sha...  66.6 us
    unnamed x2, local copies, waits for them, and re-layouts  2.02 us

profile of v3, /device:TPU:8, one launch (start us, length us, event | category | flops | bytes accessed | tf_op | source)
XLA Modules:
  0.0 69.3 jit_solution(9685816965308104959)
XLA Ops:
  0.6 66.6 %shard_map.104 = (f32[1,4,384,256]{3,2,1,0:T(8,128)S(1)}, f32[1,4,384,128]{3,2,1,0:T(8,128)S(1)}) custom-call(f32[1,4,384,256]{3,2,1,0:T(8,128)} %msa_hbm.1, f32[1,4,384,128]{3,2,1,0:T(8,128)} %pair_hbm.1, bf16[1,256,1024]{2,1,0:T(8,128)(2,1)} %weights_hbm.1, bf16[1,256,256]{2,1,0:T(8,128)(2,1)} %w_out_hbm.1, bf16[8,128]{1,0:T(8,128)(2,1)} %bitcast.3, ...), custom_call_target="tpu_custom_call" | custom-call | tf_op jit(solution)/shard_map/pallas_call | solution.py:548
  67.3 1.1 %copy.13 = f32[1,4,384,256]{3,2,1,0:T(8,128)} copy(f32[1,4,384,256]{3,2,1,0:T(8,128)S(1)} %get-tuple-element.4) | data formatting | bytes 3145728
  68.4 0.9 %copy.14 = f32[1,4,384,128]{3,2,1,0:T(8,128)} copy(f32[1,4,384,128]{3,2,1,0:T(8,128)S(1)} %get-tuple-element.5) | data formatting | bytes 1572864

commit v4 on v3

--- a/solution.py
+++ b/solution.py
@@ -135,6 +135,7 @@
     leg_send,
     leg_recv,
     pass_send,
+    entered,
 ):
     rows, n = x_sc.shape[0], x_sc.shape[1]
     n_right = nz // 2
@@ -148,6 +149,8 @@
     base = d - 2 * z
     z_right = base + 2 * lax.rem(z + 1, nz)
     z_left = base + 2 * lax.rem(z + nz - 1, nz)
+    z_right2 = base + 2 * lax.rem(z + 2, nz)
+    z_left2 = base + 2 * lax.rem(z + nz - 2, nz)
     x_right = lax.rem(d + 2 * nz, ndap)
     x_left = lax.rem(d + ndap - 2 * nz, ndap)
     x_far = lax.rem(d + 4 * nz, ndap)
@@ -188,8 +191,6 @@
 
     barrier = pltpu.get_barrier_semaphore()
     peers = (
-        (z_right, s),
-        (z_left, s),
         (x_right, s),
         (x_left, s),
         (x_far, s),
@@ -207,7 +208,33 @@
         pl.semaphore_signal(barrier, inc=1, device_id=relay_to, device_id_type=MESH)
         pl.semaphore_signal(barrier, inc=1, device_id=last_stop, device_id_type=MESH)
 
-    pl.semaphore_wait(barrier, len(peers) + 2 * core)
+    along = (
+        (z_right, z == nz - 1, 2),
+        (z_right2, z >= nz - 2, 3),
+        (z_left, z >= 1, 0),
+        (z_left2, z >= 2, 1),
+    )
+    expected = len(peers) + 2 * core
+    for peer, smaller, _ in along:
+        expected = expected + jnp.where(smaller, 1, 0)
+
+        @pl.when(jnp.logical_not(smaller))
+        def _(peer=peer):
+            pl.semaphore_signal(barrier, inc=1, device_id=(peer, s), device_id_type=MESH)
+
+    pl.semaphore_wait(barrier, expected)
+    for peer, smaller, mark in along:
+
+        @pl.when(smaller)
+        def _(peer=peer, mark=mark):
+            pl.semaphore_signal(
+                entered.at[mark], inc=1, device_id=(peer, s), device_id_type=MESH
+            )
+
+    def await_entry(index):
+        @pl.when(jnp.logical_not(along[index][1]))
+        def _():
+            pl.semaphore_wait(entered.at[index], 1)
 
     def remote(src, dst, send, recv, peer):
         return pltpu.make_async_remote_copy(
@@ -316,10 +343,10 @@
         return remote(bias.at[block], bias.at[block], send.at[t], recv.at[t], (peer, s))
 
     def z_right_copy(t, block):
-        return block_copy(zr_send, zr_recv, t, block, z_right)
+        return block_copy(zr_send, zr_recv, t - 1, block, z_right if t % 2 else z_right2)
 
     def z_left_copy(t, block):
-        return block_copy(zl_send, zl_recv, t, block, z_left)
+        return block_copy(zl_send, zl_recv, t - 1, block, z_left if t % 2 else z_left2)
 
     def x_right_copy(t, block):
         return block_copy(xr_send, xr_recv, t, block, x_right)
@@ -331,86 +358,71 @@
         return block_copy(far_send, far_recv, 0, block, x_far)
 
     def far_right_copy(t, block):
-        return block_copy(fr_send, fr_recv, t, block, z_right)
+        return block_copy(fr_send, fr_recv, t - 1, block, z_right if t % 2 else z_right2)
 
     def far_left_copy(t, block):
-        return block_copy(fl_send, fl_recv, t, block, z_left)
+        return block_copy(fl_send, fl_recv, t - 1, block, z_left if t % 2 else z_left2)
+
+    def send_on(right, left, at, below, above):
+        for t in (at + 2, at + 1):
+            if t <= n_right and below is not None:
+                right(t, below).start()
+            if t <= n_left and above is not None:
+                left(t, above).start()
+
+    def beside(index, block):
+        x_right_copy(index, block).start()
+        x_left_copy(index, block).start()
 
     far_copy(own).start()
-    z_right_copy(0, own).start()
-    z_left_copy(0, own).start()
-    x_right_copy(0, own).start()
-    x_left_copy(0, own).start()
-
-    def far_step(t):
-        below = slot(2, -t)
-        far_right_copy(t - 1, below).wait_recv()
-
-        @pl.when(t < n_right)
-        def _():
-            far_right_copy(t, below).start()
-
-        @pl.when(t <= n_left)
-        def _():
-            above = slot(2, t)
-            far_left_copy(t - 1, above).wait_recv()
-
-            @pl.when(t < n_left)
-            def _():
-                far_left_copy(t, above).start()
-
-    def gather_step(t, carry):
-        block = slot(0, -t)
-        z_right_copy(t - 1, block).wait_recv()
-
-        @pl.when(t < n_right)
-        def _():
-            z_right_copy(t, block).start()
-
-        x_right_copy(t, block).start()
-        x_left_copy(t, block).start()
-
-        @pl.when(t <= n_left)
-        def _():
-            above = slot(0, t)
-            z_left_copy(t - 1, above).wait_recv()
-
-            @pl.when(t < n_left)
-            def _():
-                z_left_copy(t, above).start()
-
-            x_right_copy(n_right + t, above).start()
-            x_left_copy(n_right + t, above).start()
-
-        @pl.when(t == 1)
-        def _():
+    beside(0, own)
+    await_entry(0)
+    await_entry(1)
+    send_on(z_right_copy, z_left_copy, 0, own, None)
+    await_entry(2)
+    await_entry(3)
+    send_on(z_right_copy, z_left_copy, 0, None, own)
+
+    def far_round(at):
+        for t in (at + 2, at + 1):
+            if t <= n_right:
+                far_right_copy(t, slot(2, -t)).wait_recv()
+                if t % 2 == 0:
+                    send_on(far_right_copy, far_left_copy, t, slot(2, -t), None)
+            if t <= n_left:
+                far_left_copy(t, slot(2, t)).wait_recv()
+                if t % 2 == 0:
+                    send_on(far_right_copy, far_left_copy, t, None, slot(2, t))
+
+    def near_round(at):
+        for t in (at + 2, at + 1):
+            if t <= n_right:
+                z_right_copy(t, slot(0, -t)).wait_recv()
+                if t % 2 == 0:
+                    send_on(z_right_copy, z_left_copy, t, slot(0, -t), None)
+                beside(t, slot(0, -t))
+            if t <= n_left:
+                z_left_copy(t, slot(0, t)).wait_recv()
+                if t % 2 == 0:
+                    send_on(z_right_copy, z_left_copy, t, None, slot(0, t))
+                beside(n_right + t, slot(0, t))
+
+    last = (n_right - 1) // 2 * 2
+    for at in range(0, last + 1, 2):
+        near_round(at)
+        if at == 0:
             far = slot(2, 0)
             far_copy(far).wait_recv()
-            far_right_copy(0, far).start()
-            far_left_copy(0, far).start()
-
-        @pl.when(t > 1)
-        def _():
-            far_step(t - 1)
-
-        @pl.when(t == 1)
-        def _():
-            relay_step(0)
-
-        @pl.when((t == 2) & (core == 1))
-        def _():
-            msa_copy(3).start()
-
-        @pl.when(t == 4)
-        def _():
-            relay_step(1)
-
-        return carry
-
-    lax.fori_loop(1, n_right + 1, gather_step, 0)
-    far_step(n_right)
-    relay_step(2)
-
+            send_on(far_right_copy, far_left_copy, 0, far, far)
+
+            @pl.when(core == 1)
+            def _():
+                msa_copy(3).start()
+
+        else:
+            far_round(at - 2)
+            relay_step(at // 2 - 1)
+    far_round(last)
     @pl.when(core == 1)
     def _():
         pair_copy(0).start()
@@ -434,6 +446,7 @@
         return carry
 
     lax.fori_loop(0, rows - 1, prepare, 0)
+    relay_step(2)
 
     def finish(t, carry):
         below, above = jnp.where(t > n_right, 0, t), jnp.where(t > n_right, t - n_right, 0)
@@ -475,16 +488,6 @@
     shard_copy(0, low, (d, s_next)).wait_send()
     shard_copy(1, low, (other, s_next)).wait_send()
 
-    def drain_z_right(t, carry):
-        z_right_copy(t, own).wait_send()
-        far_right_copy(t, own).wait_send()
-        return carry
-
-    def drain_z_left(t, carry):
-        z_left_copy(t, own).wait_send()
-        far_left_copy(t, own).wait_send()
-        return carry
-
     def drain_x(t, carry):
         x_right_copy(t, own).wait_send()
         x_left_copy(t, own).wait_send()
@@ -498,8 +501,12 @@
         out_copy(r).wait()
         return carry
 
-    lax.fori_loop(0, n_right, drain_z_right, 0)
-    lax.fori_loop(0, n_left, drain_z_left, 0)
+    for t in range(1, n_right + 1):
+        z_right_copy(t, own).wait_send()
+        far_right_copy(t, own).wait_send()
+    for t in range(1, n_left + 1):
+        z_left_copy(t, own).wait_send()
+        far_left_copy(t, own).wait_send()
     lax.fori_loop(0, nz, drain_x, 0)
     far_copy(own).wait_send()
     lax.fori_loop(0, rows, drain_rows, 0)
@@ -599,6 +606,7 @@
             dma((rows - 1,)),
             dma((rows - 1,)),
             dma((rows - 1,)),
+            pltpu.SemaphoreType.REGULAR((4,)),
         ],
         compiler_params=pltpu.CompilerParams(
             collective_id=0, has_side_effects=True, vmem_limit_bytes=44 << 20

time: 69.4 us -> 64.8 us (0.934)
  the two profiles are of different devices: /device:TPU:8 before, /device:TPU:3 now
where the time goes in v4:
time: 64.8 us; the launch traced here: 64.6 us
  Pallas kernels  62 us (96%)
  local copies, waits for them, and re-layouts  2.02 us (3%)
    pallas_call x1, Pallas kernels, body(): pl.pallas_call(functools.partial(kernel, NX, nz, ns, heads, dim), out_sha...  62 us
    unnamed x2, local copies, waits for them, and re-layouts  2.02 us

profile of v4, /device:TPU:3, one launch (start us, length us, event | category | flops | bytes accessed | tf_op | source)
XLA Modules:
  0.0 64.6 jit_solution(8964953112639312067)
XLA Ops:
  0.6 62.0 %shard_map.104 = (f32[1,4,384,256]{3,2,1,0:T(8,128)S(1)}, f32[1,4,384,128]{3,2,1,0:T(8,128)S(1)}) custom-call(f32[1,4,384,256]{3,2,1,0:T(8,128)} %msa_hbm.1, f32[1,4,384,128]{3,2,1,0:T(8,128)} %pair_hbm.1, bf16[1,256,1024]{2,1,0:T(8,128)(2,1)} %weights_hbm.1, bf16[1,256,256]{2,1,0:T(8,128)(2,1)} %w_out_hbm.1, bf16[8,128]{1,0:T(8,128)(2,1)} %bitcast.3, ...), custom_call_target="tpu_custom_call" | custom-call | tf_op jit(solution)/shard_map/pallas_call | solution.py:555
  62.6 1.1 %copy.13 = f32[1,4,384,256]{3,2,1,0:T(8,128)} copy(f32[1,4,384,256]{3,2,1,0:T(8,128)S(1)} %get-tuple-element.4) | data formatting | bytes 3145728
  63.8 0.9 %copy.14 = f32[1,4,384,128]{3,2,1,0:T(8,128)} copy(f32[1,4,384,128]{3,2,1,0:T(8,128)S(1)} %get-tuple-element.5) | data formatting | bytes 1572864

commit v5 on v4

--- a/solution.py
+++ b/solution.py
@@ -407,6 +407,24 @@
                     send_on(z_right_copy, z_left_copy, t, None, slot(0, t))
                 beside(n_right + t, slot(0, t))
 
+    for copy in fetched:
+        copy.wait()
+
+    def prepare(r, carry):
+        @pl.when(r == 0)
+        def _():
+            head_copy(0).wait_recv()
+            head_copy(1).wait_recv()
+
+        @pl.when(r > 0)
+        def _():
+            msa_copy(r).wait_recv()
+
+        prepare_row(
+            r, x_sc[r], w_sc, gain_sc[...], offset_sc[...], q_sc, k_sc, v_sc, gate_sc, heads, dim
+        )
+        return carry
+
     last = (n_right - 1) // 2 * 2
     for at in range(0, last + 1, 2):
         near_round(at)
@@ -422,31 +440,14 @@
         else:
             far_round(at - 2)
             relay_step(at // 2 - 1)
+            if at == 2:
+                prepare(0, 0)
     far_round(last)
     @pl.when(core == 1)
     def _():
         pair_copy(0).start()
 
-    for copy in fetched:
-        copy.wait()
-
-    def prepare(r, carry):
-        @pl.when(r == 0)
-        def _():
-            head_copy(0).wait_recv()
-            head_copy(1).wait_recv()
-
-        @pl.when(r > 0)
-        def _():
-            msa_copy(r).wait_recv()
-
-        prepare_row(
-            r, x_sc[r], w_sc, gain_sc[...], offset_sc[...], q_sc, k_sc, v_sc, gate_sc, heads, dim
-        )
-        return carry
-
-    lax.fori_loop(0, rows - 1, prepare, 0)
-    relay_step(2)
+    lax.fori_loop(1, rows - 1, prepare, 0)
 
     def finish(t, carry):
         below, above = jnp.where(t > n_right, 0, t), jnp.where(t > n_right, t - n_right, 0)
@@ -463,6 +464,10 @@
         @pl.when(r == rows - 1)
         def _():
             prepare(r, 0)
+
+        @pl.when(r == 1)
+        def _():
+            relay_step(2)
 
         x_sc[r] = attend_row(
             r,

time: 64.8 us -> 62.8 us (0.969)
  the two profiles are of different devices: /device:TPU:3 before, /device:TPU:54 now
where the time goes in v5:
time: 62.8 us; the launch traced here: 62.6 us
  Pallas kernels  60 us (96%)
  local copies, waits for them, and re-layouts  2.02 us (3%)
  between operations  0.64 us (1%)
    pallas_call x1, Pallas kernels, body(): pl.pallas_call(functools.partial(kernel, NX, nz, ns, heads, dim), out_sha...  60 us
    unnamed x2, local copies, waits for them, and re-layouts  2.02 us

profile of v5, /device:TPU:54, one launch (start us, length us, event | category | flops | bytes accessed | tf_op | source)
XLA Modules:
  0.0 62.6 jit_solution(16397070858847084764)
XLA Ops:
  0.6 60.0 %shard_map.104 = (f32[1,4,384,256]{3,2,1,0:T(8,128)S(1)}, f32[1,4,384,128]{3,2,1,0:T(8,128)S(1)}) custom-call(f32[1,4,384,256]{3,2,1,0:T(8,128)} %msa_hbm.1, f32[1,4,384,128]{3,2,1,0:T(8,128)} %pair_hbm.1, bf16[1,256,1024]{2,1,0:T(8,128)(2,1)} %weights_hbm.1, bf16[1,256,256]{2,1,0:T(8,128)(2,1)} %w_out_hbm.1, bf16[8,128]{1,0:T(8,128)(2,1)} %bitcast.3, ...), custom_call_target="tpu_custom_call" | custom-call | tf_op jit(solution)/shard_map/pallas_call | solution.py:560
  60.6 1.1 %copy.13 = f32[1,4,384,256]{3,2,1,0:T(8,128)} copy(f32[1,4,384,256]{3,2,1,0:T(8,128)S(1)} %get-tuple-element.4) | data formatting | bytes 3145728
  61.8 0.9 %copy.14 = f32[1,4,384,128]{3,2,1,0:T(8,128)} copy(f32[1,4,384,128]{3,2,1,0:T(8,128)S(1)} %get-tuple-element.5) | data formatting | bytes 1572864
